TPU v7x, 128 devices: a whole 4x4x4 slice. The times are simulated.
128 devices in a mesh: group: 2 (over y_hi), win: 16 (over x, y_lo, core), mp: 4 (over z).
Axes of the slice: x: 4, y: 4 (y_hi: 2, y_lo: 2; y = y_hi * 2 + y_lo), z: 4, core: 2. Of those that a mesh axis runs over, the one named last changes fastest.
Arguments:
- tokens: bfloat16 [2, 4096, 4096], P('group', 'win', 'mp'), may hold values from -7 to 7, as said below
- proj: bfloat16 [2, 4096, 4096], P('group', None, 'mp'), may hold values from -1 to 1, as said below
- cotangent: bfloat16 [4096, 4096], P('win', 'mp'), may hold values from -6 to 6
- counts: int32 [16], P('win'), may hold values from 64 to 256, as said below
- frames: int32 [4096], P('win'), may hold values from 0 to 3, as said below
Outputs:
- input_grads: bfloat16 [2, 4096, 4096], P('group', 'win', 'mp')
- weight_grads: float32 [2, 4096, 4096], P('group', 'win', 'mp')
Inputs may be any that keep to these rules, and one draw needn't show every extreme that they name: Every value lies within the range; proj slot 0 entries scale as 1 / sqrt(1024), slot 1 as 1 / sqrt(4096). `tokens`: finite values. `counts`: some window has all 256 slots live and some window exactly 64. Each window has a token that sees only the first frame and one that sees all frames.
All inputs are finite; a program needn't handle non-finite values.
Results may differ from a plain program's by a relative error of at most 0.015.
The roundings to bfloat16 on the way count: a program that leaves them out, or rounds other values in their place, can miss the bound.
Values may be sent and summed in bfloat16 or wider, within the bound.
A program may use at most 192 MiB of HBM per device.

v0:
```python
import jax
import jax.numpy as jnp
from jax import lax
from jax.sharding import PartitionSpec as P

DV = 1024
HEAD_DIM = 128
FRAMES = 4


def from_behind(shard, axis, by):
    devices = lax.axis_size(axis)
    pairs = [(i, i + by) for i in range(devices) if 0 <= i + by < devices]
    return lax.ppermute(shard, axis, pairs)


def one_head(head_items, allowed):
    queries, key_rows, value_rows, upstream = head_items
    factor = HEAD_DIM ** (-0.5)
    scores = jnp.einsum("qd,kd->qk", queries, key_rows, preferred_element_type=jnp.float32) * factor
    scores = jnp.where(allowed, scores, -1e30)
    top_score = jnp.max(scores, axis=-1, keepdims=True)
    shifted = jnp.exp(scores - top_score)
    attention = shifted / jnp.sum(shifted, axis=-1, keepdims=True)
    rounded = attention.astype(jnp.bfloat16)
    value_grad = jnp.einsum(
        "qk,qd->kd", rounded, upstream, preferred_element_type=jnp.float32
    ).astype(jnp.bfloat16)
    attn_grad = jnp.einsum("qd,kd->qk", upstream, value_rows, preferred_element_type=jnp.float32)
    score_grad = (
        attention * (attn_grad - jnp.sum(attention * attn_grad, axis=-1, keepdims=True)) * factor
    )
    score_grad = score_grad.astype(jnp.bfloat16)
    query_grad = jnp.einsum(
        "qk,kd->qd", score_grad, key_rows, preferred_element_type=jnp.float32
    ).astype(jnp.bfloat16)
    key_grad = jnp.einsum(
        "qk,qd->kd", score_grad, queries, preferred_element_type=jnp.float32
    ).astype(jnp.bfloat16)
    return (query_grad, key_grad, value_grad)


def head_grads(queries, key_rows, value_rows, upstream, allowed):
    head_count = queries.shape[1] // HEAD_DIM

    def split_heads(array):
        return array.reshape(array.shape[0], head_count, HEAD_DIM).transpose(1, 0, 2)

    def merge_heads(array):
        return array.transpose(1, 0, 2).reshape(array.shape[1], head_count * HEAD_DIM)

    def per_head(head_items):
        return one_head(head_items, allowed)

    query_grad, key_grad, value_grad = lax.map(
        per_head,
        (
            split_heads(queries),
            split_heads(key_rows),
            split_heads(value_rows),
            split_heads(upstream),
        ),
    )
    return (merge_heads(query_grad), merge_heads(key_grad), merge_heads(value_grad))


def local(tokens, proj, cotangent, counts, frames):
    group_index = lax.axis_index("group")
    is_video = group_index == 0
    local_rows = tokens[0]
    weight = proj[0]
    row_count = local_rows.shape[0]
    columns = weight.shape[1]
    full_width = weight.shape[0]
    video_rows = row_count * full_width // DV
    gathered = lax.all_gather(local_rows, "mp", axis=1, tiled=True)
    features = gathered.reshape(video_rows, DV)
    w_key = weight[:DV]
    w_value = weight[DV : 2 * DV]

    def video_front():
        key_rows = jnp.dot(features, w_key, preferred_element_type=jnp.float32).astype(jnp.bfloat16)
        value_rows = jnp.dot(features, w_value, preferred_element_type=jnp.float32).astype(
            jnp.bfloat16
        )
        return (
            jnp.concatenate([key_rows, value_rows], 1),
            jnp.zeros((row_count, columns), jnp.bfloat16),
        )

    def neural_front():
        queries = jnp.dot(gathered, weight, preferred_element_type=jnp.float32).astype(jnp.bfloat16)
        return (jnp.zeros((video_rows, 2 * columns), jnp.bfloat16), queries)

    outgoing, queries = lax.cond(is_video, video_front, neural_front)
    arrived = from_behind(outgoing, "group", 1)
    key_rows = arrived[:, :columns]
    value_rows = arrived[:, columns:]
    live_rows = lax.iota(jnp.int32, row_count) < counts[0]
    upstream = jnp.where(live_rows[:, None], cotangent, jnp.zeros_like(cotangent))
    key_frame = lax.iota(jnp.int32, video_rows) // (video_rows // FRAMES)
    allowed = key_frame[None, :] <= frames[:, None]

    def attend():
        return head_grads(queries, key_rows, value_rows, upstream, allowed)

    def neural_input(query_grad):
        return jnp.dot(query_grad, weight.T, preferred_element_type=jnp.float32)

    def neural_weight(query_grad):
        return jnp.dot(gathered.T, query_grad, preferred_element_type=jnp.float32)

    def neural_all():
        query_grad, key_grad, value_grad = attend()
        return (
            jnp.concatenate([key_grad, value_grad], 1),
            query_grad,
            neural_input(query_grad),
            neural_weight(query_grad),
        )

    def video_wait_all():
        return (
            jnp.zeros((video_rows, 2 * columns), jnp.bfloat16),
            jnp.zeros((row_count, columns), jnp.bfloat16),
            jnp.zeros((row_count, full_width), jnp.float32),
            jnp.zeros((full_width, columns), jnp.float32),
        )

    returning, query_grad, early_input, early_weight = lax.cond(
        is_video, video_wait_all, neural_all
    )
    returned = from_behind(returning, "group", -1)

    def video_back():
        key_grad = returned[:, :columns]
        value_grad = returned[:, columns:]
        feature_part = jnp.dot(key_grad, w_key.T, preferred_element_type=jnp.float32)
        feature_part = feature_part + jnp.dot(
            value_grad, w_value.T, preferred_element_type=jnp.float32
        )
        feature_part = feature_part.reshape(row_count, full_width)
        weight_part = jnp.concatenate(
            [
                jnp.dot(features.T, key_grad, preferred_element_type=jnp.float32),
                jnp.dot(features.T, value_grad, preferred_element_type=jnp.float32),
                jnp.zeros((full_width - 2 * DV, columns), jnp.float32),
            ],
            0,
        )
        return (feature_part, weight_part)

    def neural_back():
        return (early_input, early_weight)

    input_part, weight_part = lax.cond(is_video, video_back, neural_back)
    summed = lax.psum_scatter(
        input_part.astype(jnp.bfloat16), "mp", scatter_dimension=1, tiled=True
    ).astype(jnp.float32)
    residual = jnp.where(is_video, jnp.zeros_like(summed), cotangent.astype(jnp.float32))
    input_grads = (summed + residual).astype(jnp.bfloat16)
    weight_grads = lax.psum_scatter(weight_part, "win", scatter_dimension=0, tiled=True)
    return (input_grads[None], weight_grads[None])


def solution(mesh):
    return jax.shard_map(
        local,
        mesh=mesh,
        in_specs=(
            P("group", "win", "mp"),
            P("group", None, "mp"),
            P("win", "mp"),
            P("win"),
            P("win"),
        ),
        out_specs=(P("group", "win", "mp"), P("group", "win", "mp")),
        check_vma=False,
    )
```

profile of v0, /device:TPU:1, one launch (start us, length us, event | category | flops | bytes accessed | tf_op | source)
XLA Modules:
  0.0 590.1 jit_solution(15386314961577830210)
XLA Ops:
  7.2 0.0 all-gather.3.cloned.1.call-start
  7.2 0.7 all-gather.3.cloned.1.call-update
  7.9 0.0 reduce-scatter.3.cloned.1.call-start
  8.0 4.7 slice_bitcast_fusion
  12.7 31.3 %all-gather.3.cloned.1.call-done = bf16[1,256,4096]{2,1,0:T(8,128)(2,1)} async-done(((bf16[1,256,1024]{2,1,0:T(8,128)(2,1)}), bf16[1,256,4096]{2,1,0:T(8,128)(2,1)}) %all-gather.3.cloned.1.call-update) | async-done | bytes 2097168 | tf_op jit(solution)/shard_map/all_gather | solution.py:76
  44.0 0.0 copy-start
  44.0 4.5 reshape.55
  48.5 0.0 copy-done
  48.5 0.0 copy-start.6
  48.5 0.0 copy-start.12
  48.5 8.5 %conditional.3 = (bf16[1024,2048]{0,1:T(8,128)(2,1)S(1)}, bf16[256,1024]{1,0:T(8,128)(2,1)}) conditional(s32[]{:T(128)} %convert_element_type.41, (bf16[256,4096]{1,0:T(8,128)(2,1)S(1)}, bf16[4096,1024]{1,0:T(8,128)(2,1)}) %tuple.116, (bf16[1024,1024]{1,0:T(8,128)(2,1)}, bf16[1024,1024]{1,0:T(8,128)(2,1)}, bf16[1024,1024]{1,0:T(8,128)(2,1)}) %tuple.68), branch_computations={%region_0.0_spmd, %region_1.0_spmd} | conditional | flops 4305453056 | bytes 38273096 | solution.py:95
  48.5 0.0 copy-start.3
  48.5 0.0 copy-start.7
  48.5 4.8 convolution_convert_fusion.2
  53.3 0.0 copy-done.3
  53.3 0.0 copy-done.7
  53.3 2.4 convolution_convert_fusion.1
  55.7 0.4 pad_maximum_fusion
  56.1 0.9 broadcast.66
  57.0 5.2 collective-permute-start
  62.2 87.3 %collective-permute-done = bf16[1024,2048]{0,1:T(8,128)(2,1)} collective-permute-done((bf16[1024,2048]{0,1:T(8,128)(2,1)S(1)}, bf16[1024,2048]{0,1:T(8,128)(2,1)}, u32[]{:S(2)}, u32[]{:S(2)}) %collective-permute-start) | collective-permute-done | bytes 4194336 | tf_op jit(solution)/shard_map/ppermute | solution.py:14
  149.5 0.0 copy-done.6
  149.5 0.0 copy-done.12
  149.5 8.8 %conditional.4 = (bf16[1024,2048]{1,0:T(8,128)(2,1)S(1)}, bf16[256,4096]{1,0:T(8,128)(2,1)S(1)}, f32[4096,1024]{0,1:T(8,128)}) conditional(s32[]{:T(128)} %convert_element_type.41, (bf16[256,1024]{1,0:T(8,128)(2,1)}, bf16[1024,2048]{0,1:T(8,128)(2,1)}, s32[1]{0:T(128)}, s32[256,1]{0,1:T(1,128)S(1)}, bf16[256,1024]{1,0:T(8,128)(2,1)S(1)}, ...), branch_computations={%region_2.8_spmd, %region_8.9_spmd} | conditional | flops 4644445696 | bytes 113604480 | solution.py:130
  149.7 0.2 broadcast.72
  149.9 0.5 broadcast.71
  150.4 7.9 %broadcast.73 = f32[4096,1024]{0,1:T(8,128)} broadcast(f32[]{:T(128)} %constant.80.clone), dimensions={} | broadcast | bytes 16777220 | tf_op jit(solution)/shard_map/broadcast.14
  158.3 0.0 copy-start.5
  158.3 1.3 collective-permute-start.1
  159.6 176.7 %collective-permute-done.1 = bf16[1024,2048]{1,0:T(8,128)(2,1)S(1)} collective-permute-done((bf16[1024,2048]{1,0:T(8,128)(2,1)S(1)}, bf16[1024,2048]{1,0:T(8,128)(2,1)S(1)}, u32[]{:S(2)}, u32[]{:S(2)}) %collective-permute-start.1) | collective-permute-done | bytes 4194336 | tf_op jit(solution)/shard_map/ppermute | solution.py:14
  336.3 0.0 copy-done.5
  336.3 34.7 %conditional.5 = (bf16[256,4096]{1,0:T(8,128)(2,1)}, f32[4096,1024]{1,0:T(8,128)}) conditional(s32[]{:T(128)} %convert_element_type.41, (bf16[256,4096]{1,0:T(8,128)(2,1)}, f32[4096,1024]{0,1:T(8,128)}) %tuple.118, (bf16[1024,2048]{1,0:T(8,128)(2,1)S(1)}, bf16[1024,1024]{1,0:T(8,128)(2,1)}, bf16[1024,1024]{1,0:T(8,128)(2,1)}, ...), branch_computations={%region_9.10_spmd, %region_10.11_spmd} | conditional | flops 8600420352 | bytes 115392640 | solution.py:156
  336.3 0.0 copy-start.10
  336.3 0.0 copy-start.8
  336.4 5.5 fusion.7
  341.9 0.0 copy-done.10
  341.9 0.0 copy-done.8
  341.9 3.7 convolution_add_fusion
  345.6 0.0 copy-start.4
  345.6 4.5 reshape.53
  350.1 0.0 copy-done.4
  350.1 0.0 copy-start.11
  350.1 6.2 %fusion.2 = f32[1024,1024]{1,0:T(8,128)} fusion(bf16[1024,1024]{1,0:T(8,128)(2,1)S(1)} %copy-done.4, bf16[1024,2048]{1,0:T(8,128)(2,1)} %copy-done.10), kind=kOutput, calls=%fused_computation.7 | convolution fusion | flops 2147483648 | bytes 8388608 | tf_op jit(solution)/shard_map/cond/branch_1_fun/dot_general | solution.py:146
  356.3 0.0 copy-done.11
  356.3 4.4 fusion.5
  360.7 10.3 %maximum_maximum_fusion = f32[4096,1024]{1,0:T(8,128)} fusion(f32[1024,1024]{1,0:T(8,128)} %fusion.2, f32[1024,1024]{1,0:T(8,128)} %fusion.5, f32[4096]{0:T(1024)S(1)} %pad.4.clone), kind=kLoop, calls=%fused_computation.5 | loop fusion | flops 8388608 | bytes 25182208 | tf_op jit(solution)/shard_map/cond/branch_1_fun/concatenate | solution.py:143
  371.0 0.0 reduce-scatter.3.cloned.1.call-update
  371.0 0.0 reduce-scatter.5.cloned.1.call-start
  371.1 0.7 reduce-scatter.5.cloned.1.call-update
  371.8 28.4 %reduce-scatter.3.cloned.1.call-done = bf16[256,1024]{1,0:T(8,128)(2,1)} async-done(((bf16[256,4096]{1,0:T(8,128)(2,1)}), bf16[256,1024]{1,0:T(8,128)(2,1)}) %reduce-scatter.3.cloned.1.call-update) | async-done | bytes 524304 | tf_op jit(solution)/shard_map/reduce_scatter | solution.py:157
  400.2 2.0 fusion.39
  402.2 181.4 %reduce-scatter.5.cloned.1.call-done = f32[256,1024]{1,0:T(8,128)} async-done(((f32[4096,1024]{1,0:T(8,128)}), f32[256,1024]{1,0:T(8,128)}) %reduce-scatter.5.cloned.1.call-update) | async-done | bytes 1048592 | tf_op jit(solution)/shard_map/reduce_scatter | solution.py:162
  (4 shorter events, 0.0 us)
Async XLA Ops:
  7.2 36.8 %all-gather.3.cloned.1.call-start = ((), (), s32[]{:S(2)}) async-start(), calls=%async_computation.4 | async-start | bytes 2621440 | tf_op jit(solution)/shard_map/all_gather | solution.py:76
  7.9 392.3 %reduce-scatter.3.cloned.1.call-start = ((), (), s32[]{:S(2)}) async-start(), calls=%async_computation.2 | async-start | bytes 2621440 | tf_op jit(solution)/shard_map/reduce_scatter | solution.py:157
  44.0 4.5 copy-start
  48.5 101.0 %copy-start.6 = (bf16[256,1024]{1,0:T(8,128)(2,1)S(1)}, bf16[256,1024]{1,0:T(8,128)(2,1)}, u32[]{:S(2)}) copy-start(bf16[256,1024]{1,0:T(8,128)(2,1)} %param.15) | copy-start | bytes 1572868
  48.5 101.0 %copy-start.12 = (s32[256]{0:T(256)S(1)}, s32[256]{0:T(256)}, u32[]{:S(2)}) copy-start(s32[256]{0:T(256)} %param.17) | copy-start | bytes 3076
  48.5 4.8 copy-start.3
  48.5 4.8 copy-start.7
  57.0 92.5 %collective-permute-start = (bf16[1024,2048]{0,1:T(8,128)(2,1)S(1)}, bf16[1024,2048]{0,1:T(8,128)(2,1)}, u32[]{:S(2)}, u32[]{:S(2)}) collective-permute-start(bf16[1024,2048]{0,1:T(8,128)(2,1)S(1)} %get-tuple-element.207), channel_id=1, source_target_pairs={{0,64},{1,65},{2,66},{3,67},{4,68},{5,69},{6,70},{7,71},{8,72},{9,... | collective-permute-start | bytes 12582920 | tf_op jit(solution)/shard_map/ppermute | solution.py:14
  158.3 178.0 %copy-start.5 = (bf16[256,4096]{1,0:T(8,128)(2,1)}, bf16[256,4096]{1,0:T(8,128)(2,1)S(1)}, u32[]{:S(2)}) copy-start(bf16[256,4096]{1,0:T(8,128)(2,1)S(1)} %get-tuple-element.208) | copy-start | bytes 6291460
  158.3 178.0 %collective-permute-start.1 = (bf16[1024,2048]{1,0:T(8,128)(2,1)S(1)}, bf16[1024,2048]{1,0:T(8,128)(2,1)S(1)}, u32[]{:S(2)}, u32[]{:S(2)}) collective-permute-start(bf16[1024,2048]{1,0:T(8,128)(2,1)S(1)} %get-tuple-element.210), channel_id=1, source_target_pairs={{64,0},{65,1},{66,2},{67,3},{68,4},{69,5},{70,6},{71,7},{72,8},{73... | collective-permute-start | bytes 12582920 | tf_op jit(solution)/shard_map/ppermute | solution.py:14
  336.3 5.5 copy-start.10
  336.3 5.5 copy-start.8
  345.6 4.5 copy-start.4
  350.1 6.2 %copy-start.11 = (bf16[1024,2048]{1,0:T(8,128)(2,1)S(1)}, bf16[1024,2048]{1,0:T(8,128)(2,1)}, u32[]{:S(2)}) copy-start(bf16[1024,2048]{1,0:T(8,128)(2,1)} %copy-done.10) | copy-start | bytes 12582916 | tf_op jit(solution)/shard_map/cond
  371.0 212.6 %reduce-scatter.5.cloned.1.call-start = ((), (), s32[]{:S(2)}) async-start(), calls=%async_computation.3 | async-start | bytes 17825792 | tf_op jit(solution)/shard_map/reduce_scatter | solution.py:162
Sparse Core Ops, SparseCore 0:
  9.7 34.2 all-gather.2
  371.2 28.9 reduce-scatter.2
  403.3 180.2 reduce-scatter.4
where the time goes:
time: 592 us; the launch traced here: 590 us
  waiting for transfers between devices  506 us (85%)
  matrix products  26.9 us (5%)
  local copies, waits for them, and re-layouts  23.3 us (4%)
  between operations  13.8 us (2%)
  other arithmetic  12.8 us (2%)
  starting transfers between devices  6.59 us (1%)
    ppermute x2, waiting for transfers between devices, from_behind(): return lax.ppermute(shard, axis, pairs)  264 us
    reduce_scatter x1, waiting for transfers between devices, local(): lax.psum_scatter(weight_part, 'win', scatter_dimension=0, tiled=True)  181 us
    all_gather x1, waiting for transfers between devices, local(): gathered = lax.all_gather(local_rows, 'mp', axis=1, tiled=True)  31.3 us
    reduce_scatter x1, waiting for transfers between devices, local(): lax.psum_scatter(input_part.astype(jnp.bfloat16), 'mp', scatter_dimension...  28.4 us
  transfers between devices with their start and end apart: 5, of which 5 were waited for; matrix products, arithmetic and copies ran while one was open for 1% of the time, Pallas kernels for 0%

commit v1 on v0

--- a/solution.py
+++ b/solution.py
@@ -6,6 +6,16 @@
 DV = 1024
 HEAD_DIM = 128
 FRAMES = 4
+
+
+def gather_by_hops(x, axis, dim):
+    n_dev = lax.axis_size(axis)
+    held, blocks = (x, [x])
+    for _ in range(n_dev - 1):
+        held = lax.ppermute(held, axis, [(i, (i + 1) % n_dev) for i in range(n_dev)])
+        blocks.insert(0, held)
+    line = jnp.concatenate(blocks, axis=dim)
+    return jnp.roll(line, (lax.axis_index(axis) + 1) * x.shape[dim], axis=dim)
 
 
 def from_behind(shard, axis, by):
@@ -73,7 +83,7 @@
     columns = weight.shape[1]
     full_width = weight.shape[0]
     video_rows = row_count * full_width // DV
-    gathered = lax.all_gather(local_rows, "mp", axis=1, tiled=True)
+    gathered = gather_by_hops(local_rows, "mp", 1)
     features = gathered.reshape(video_rows, DV)
     w_key = weight[:DV]
     w_value = weight[DV : 2 * DV]

time: 592 us -> 593 us (level)
    ppermute x0 -> x3, waiting for transfers between devices: none -> 35.1 us  [gather_by_hops(): lax.ppermute(held, axis, [(i, (i + 1) % n_dev) for i in range(n_dev)])]
    all_gather x1 -> x0, waiting for transfers between devices: 31.3 us -> none  [local(): gathered = lax.all_gather(local_rows, 'mp', axis=1, tiled=True)]
  transfers between devices with their start and end apart: 5 -> 7, of which waited for: 5 -> 7; matrix products, arithmetic and copies ran while one was open for 1% -> 1% of each run, Pallas kernels for 0% -> 0%
where the time goes in v1:
time: 593 us; the launch traced here: 591 us
  waiting for transfers between devices  506 us (85%)
  matrix products  26.9 us (5%)
  local copies, waits for them, and re-layouts  21.8 us (4%)
  between operations  14.1 us (2%)
  other arithmetic  12.8 us (2%)
  starting transfers between devices  9.29 us (2%)
    ppermute x2, waiting for transfers between devices, from_behind(): return lax.ppermute(shard, axis, pairs)  259 us
    reduce_scatter x1, waiting for transfers between devices, local(): lax.psum_scatter(weight_part, 'win', scatter_dimension=0, tiled=True)  181 us
    ppermute x3, waiting for transfers between devices, gather_by_hops(): lax.ppermute(held, axis, [(i, (i + 1) % n_dev) for i in range(n_dev)])  35.1 us
    reduce_scatter x1, waiting for transfers between devices, local(): lax.psum_scatter(input_part.astype(jnp.bfloat16), 'mp', scatter_dimension...  29.7 us
  transfers between devices with their start and end apart: 7, of which 7 were waited for; matrix products, arithmetic and copies ran while one was open for 1% of the time, Pallas kernels for 0%

profile of v1, /device:TPU:1, one launch (start us, length us, event | category | flops | bytes accessed | tf_op | source)
XLA Modules:
  0.0 591.3 jit_solution(9501317238395307287)
XLA Ops:
  7.2 0.0 reduce-scatter.3.cloned.1.call-start
  7.2 2.5 collective-permute-start
  9.7 14.0 %collective-permute-done = bf16[256,1024]{1,0:T(8,128)(2,1)S(1)} collective-permute-done((bf16[256,1024]{1,0:T(8,128)(2,1)}, bf16[256,1024]{1,0:T(8,128)(2,1)S(1)}, u32[]{:S(2)}, u32[]{:S(2)}) %collective-permute-start) | collective-permute-done | bytes 524320 | tf_op jit(solution)/shard_map/ppermute | solution.py:15
  23.7 0.0 collective-permute-start.1
  23.7 13.4 %collective-permute-done.1 = bf16[256,1024]{1,0:T(8,128)(2,1)S(1)} collective-permute-done((bf16[256,1024]{1,0:T(8,128)(2,1)S(1)}, bf16[256,1024]{1,0:T(8,128)(2,1)S(1)}, u32[]{:S(2)}, u32[]{:S(2)}) %collective-permute-start.1) | collective-permute-done | bytes 524320 | tf_op jit(solution)/shard_map/ppermute | solution.py:15
  37.1 0.0 collective-permute-start.2
  37.1 4.8 slice_bitcast_fusion
  41.9 0.0 copy-start.5
  41.9 7.7 %collective-permute-done.2 = bf16[256,1024]{1,0:T(8,128)(2,1)S(1)} collective-permute-done((bf16[256,1024]{1,0:T(8,128)(2,1)S(1)}, bf16[256,1024]{1,0:T(8,128)(2,1)S(1)}, u32[]{:S(2)}, u32[]{:S(2)}) %collective-permute-start.2) | collective-permute-done | bytes 524320 | tf_op jit(solution)/shard_map/ppermute | solution.py:15
  49.7 0.0 copy-done.5
  50.0 0.1 constant_dynamic-slice_fusion
  50.1 2.6 reshape.55
  52.7 0.0 copy-start.6
  52.7 0.0 copy-start.12
  52.7 8.5 %conditional.3 = (bf16[1024,2048]{0,1:T(8,128)(2,1)S(1)}, bf16[256,1024]{1,0:T(8,128)(2,1)}) conditional(s32[]{:T(128)} %convert_element_type.41, (bf16[256,4096]{1,0:T(8,128)(2,1)S(1)}, bf16[4096,1024]{1,0:T(8,128)(2,1)}) %tuple.107, (bf16[1024,1024]{1,0:T(8,128)(2,1)}, bf16[1024,1024]{1,0:T(8,128)(2,1)}, bf16[1024,1024]{1,0:T(8,128)(2,1)}) %tuple.63), branch_computations={%region_0.1_spmd, %region_1.2_spmd} | conditional | flops 4305453056 | bytes 38273096 | solution.py:105
  52.7 0.0 copy-start.2
  52.7 0.0 copy-start.7
  52.7 4.8 convolution_convert_fusion.2
  57.5 0.0 copy-done.2
  57.5 0.0 copy-done.7
  57.5 2.4 convolution_convert_fusion.1
  59.9 0.4 pad_maximum_fusion
  60.3 0.9 broadcast.68
  61.2 5.4 collective-permute-start.3
  66.6 84.8 %collective-permute-done.3 = bf16[1024,2048]{0,1:T(8,128)(2,1)} collective-permute-done((bf16[1024,2048]{0,1:T(8,128)(2,1)S(1)}, bf16[1024,2048]{0,1:T(8,128)(2,1)}, u32[]{:S(2)}, u32[]{:S(2)}) %collective-permute-start.3) | collective-permute-done | bytes 4194336 | tf_op jit(solution)/shard_map/ppermute | solution.py:24
  151.4 0.0 copy-done.6
  151.4 0.0 copy-done.12
  151.4 8.8 %conditional.4 = (bf16[1024,2048]{1,0:T(8,128)(2,1)S(1)}, bf16[256,4096]{1,0:T(8,128)(2,1)S(1)}, f32[4096,1024]{0,1:T(8,128)}) conditional(s32[]{:T(128)} %convert_element_type.41, (bf16[256,1024]{1,0:T(8,128)(2,1)}, bf16[1024,2048]{0,1:T(8,128)(2,1)}, s32[1]{0:T(128)}, s32[256,1]{0,1:T(1,128)S(1)}, bf16[256,1024]{1,0:T(8,128)(2,1)S(1)}, ...), branch_computations={%region_2.8_spmd, %region_8.9_spmd} | conditional | flops 4644445696 | bytes 113604480 | solution.py:140
  151.6 0.2 broadcast.75
  151.9 0.5 broadcast.74
  152.4 7.9 %broadcast.76 = f32[4096,1024]{0,1:T(8,128)} broadcast(f32[]{:T(128)} %constant.100.clone), dimensions={} | broadcast | bytes 16777220 | tf_op jit(solution)/shard_map/broadcast.14
  160.3 0.0 copy-start.4
  160.3 1.3 collective-permute-start.4
  161.5 174.3 %collective-permute-done.4 = bf16[1024,2048]{1,0:T(8,128)(2,1)S(1)} collective-permute-done((bf16[1024,2048]{1,0:T(8,128)(2,1)S(1)}, bf16[1024,2048]{1,0:T(8,128)(2,1)S(1)}, u32[]{:S(2)}, u32[]{:S(2)}) %collective-permute-start.4) | collective-permute-done | bytes 4194336 | tf_op jit(solution)/shard_map/ppermute | solution.py:24
  335.9 0.0 copy-done.4
  335.9 34.7 %conditional.5 = (bf16[256,4096]{1,0:T(8,128)(2,1)}, f32[4096,1024]{1,0:T(8,128)}) conditional(s32[]{:T(128)} %convert_element_type.41, (bf16[256,4096]{1,0:T(8,128)(2,1)}, f32[4096,1024]{0,1:T(8,128)}) %tuple.109, (bf16[1024,2048]{1,0:T(8,128)(2,1)S(1)}, bf16[1024,1024]{1,0:T(8,128)(2,1)}, bf16[1024,1024]{1,0:T(8,128)(2,1)}, ...), branch_computations={%region_9.10_spmd, %region_10.11_spmd} | conditional | flops 8600420352 | bytes 115392640 | solution.py:166
  335.9 0.0 copy-start.10
  335.9 0.0 copy-start.8
  335.9 5.5 fusion.7
  341.4 0.0 copy-done.10
  341.4 0.0 copy-done.8
  341.4 3.7 convolution_add_fusion
  345.1 0.0 copy-start.3
  345.1 4.5 reshape.53
  349.6 0.0 copy-done.3
  349.6 0.0 copy-start.11
  349.6 6.2 %fusion.2 = f32[1024,1024]{1,0:T(8,128)} fusion(bf16[1024,1024]{1,0:T(8,128)(2,1)S(1)} %copy-done.3, bf16[1024,2048]{1,0:T(8,128)(2,1)} %copy-done.10), kind=kOutput, calls=%fused_computation.7 | convolution fusion | flops 2147483648 | bytes 8388608 | tf_op jit(solution)/shard_map/cond/branch_1_fun/dot_general | solution.py:156
  355.8 0.0 copy-done.11
  355.8 4.4 fusion.5
  360.2 10.3 %maximum_maximum_fusion = f32[4096,1024]{1,0:T(8,128)} fusion(f32[1024,1024]{1,0:T(8,128)} %fusion.2, f32[1024,1024]{1,0:T(8,128)} %fusion.5, f32[4096]{0:T(1024)S(1)} %pad.4.clone), kind=kLoop, calls=%fused_computation.5 | loop fusion | flops 8388608 | bytes 25182208 | tf_op jit(solution)/shard_map/cond/branch_1_fun/concatenate | solution.py:153
  370.6 0.0 reduce-scatter.3.cloned.1.call-update
  370.6 0.0 reduce-scatter.5.cloned.1.call-start
  370.6 0.7 reduce-scatter.5.cloned.1.call-update
  371.4 29.7 %reduce-scatter.3.cloned.1.call-done = bf16[256,1024]{1,0:T(8,128)(2,1)} async-done(((bf16[256,4096]{1,0:T(8,128)(2,1)}), bf16[256,1024]{1,0:T(8,128)(2,1)}) %reduce-scatter.3.cloned.1.call-update) | async-done | bytes 524304 | tf_op jit(solution)/shard_map/reduce_scatter | solution.py:167
  401.0 2.0 fusion.39
  403.1 181.4 %reduce-scatter.5.cloned.1.call-done = f32[256,1024]{1,0:T(8,128)} async-done(((f32[4096,1024]{1,0:T(8,128)}), f32[256,1024]{1,0:T(8,128)}) %reduce-scatter.5.cloned.1.call-update) | async-done | bytes 1048592 | tf_op jit(solution)/shard_map/reduce_scatter | solution.py:172
  (12 shorter events, 0.3 us)
Async XLA Ops:
  7.2 393.9 %reduce-scatter.3.cloned.1.call-start = ((), (), s32[]{:S(2)}) async-start(), calls=%async_computation.2 | async-start | bytes 2621440 | tf_op jit(solution)/shard_map/reduce_scatter | solution.py:167
  7.2 16.5 %collective-permute-start = (bf16[256,1024]{1,0:T(8,128)(2,1)}, bf16[256,1024]{1,0:T(8,128)(2,1)S(1)}, u32[]{:S(2)}, u32[]{:S(2)}) collective-permute-start(bf16[256,1024]{1,0:T(8,128)(2,1)} %bitcast.130), channel_id=1, source_target_pairs={{0,1},{1,2},{2,3},{3,0},{4,5},{5,6},{6,7},{7,4},{8,9},{9,10},{10,1... | collective-permute-start | bytes 1572872 | tf_op jit(solution)/shard_map/ppermute | solution.py:15
  23.7 13.4 %collective-permute-start.1 = (bf16[256,1024]{1,0:T(8,128)(2,1)S(1)}, bf16[256,1024]{1,0:T(8,128)(2,1)S(1)}, u32[]{:S(2)}, u32[]{:S(2)}) collective-permute-start(bf16[256,1024]{1,0:T(8,128)(2,1)S(1)} %collective-permute-done), channel_id=1, source_target_pairs={{0,1},{1,2},{2,3},{3,0},{4,5},{5,6},{6,7},{7,4},{8,9},{9,10},{10,1... | collective-permute-start | bytes 1572872 | tf_op jit(solution)/shard_map/ppermute | solution.py:15
  37.1 12.5 %collective-permute-start.2 = (bf16[256,1024]{1,0:T(8,128)(2,1)S(1)}, bf16[256,1024]{1,0:T(8,128)(2,1)S(1)}, u32[]{:S(2)}, u32[]{:S(2)}) collective-permute-start(bf16[256,1024]{1,0:T(8,128)(2,1)S(1)} %collective-permute-done.1), channel_id=1, source_target_pairs={{0,1},{1,2},{2,3},{3,0},{4,5},{5,6},{6,7},{7,4},{8,9},{9,10},{10,1... | collective-permute-start | bytes 1572872 | tf_op jit(solution)/shard_map/ppermute | solution.py:15
  41.9 7.8 %copy-start.5 = (bf16[1,256,1024]{2,1,0:T(8,128)(2,1)S(1)}, bf16[1,256,1024]{2,1,0:T(8,128)(2,1)}, u32[]{:S(2)}) copy-start(bf16[1,256,1024]{2,1,0:T(8,128)(2,1)} %param.13) | copy-start | bytes 1572868
  52.7 98.7 %copy-start.6 = (bf16[256,1024]{1,0:T(8,128)(2,1)S(1)}, bf16[256,1024]{1,0:T(8,128)(2,1)}, u32[]{:S(2)}) copy-start(bf16[256,1024]{1,0:T(8,128)(2,1)} %param.15) | copy-start | bytes 1572868
  52.7 98.7 %copy-start.12 = (s32[256]{0:T(256)S(1)}, s32[256]{0:T(256)}, u32[]{:S(2)}) copy-start(s32[256]{0:T(256)} %param.17) | copy-start | bytes 3076
  52.7 4.8 copy-start.2
  52.7 4.8 copy-start.7
  61.2 90.2 %collective-permute-start.3 = (bf16[1024,2048]{0,1:T(8,128)(2,1)S(1)}, bf16[1024,2048]{0,1:T(8,128)(2,1)}, u32[]{:S(2)}, u32[]{:S(2)}) collective-permute-start(bf16[1024,2048]{0,1:T(8,128)(2,1)S(1)} %get-tuple-element.211), channel_id=1, source_target_pairs={{0,64},{1,65},{2,66},{3,67},{4,68},{5,69},{6,70},{7,71},{8,72},{9,... | collective-permute-start | bytes 12582920 | tf_op jit(solution)/shard_map/ppermute | solution.py:24
  160.3 175.6 %copy-start.4 = (bf16[256,4096]{1,0:T(8,128)(2,1)}, bf16[256,4096]{1,0:T(8,128)(2,1)S(1)}, u32[]{:S(2)}) copy-start(bf16[256,4096]{1,0:T(8,128)(2,1)S(1)} %get-tuple-element.212) | copy-start | bytes 6291460
  160.3 175.6 %collective-permute-start.4 = (bf16[1024,2048]{1,0:T(8,128)(2,1)S(1)}, bf16[1024,2048]{1,0:T(8,128)(2,1)S(1)}, u32[]{:S(2)}, u32[]{:S(2)}) collective-permute-start(bf16[1024,2048]{1,0:T(8,128)(2,1)S(1)} %get-tuple-element.214), channel_id=1, source_target_pairs={{64,0},{65,1},{66,2},{67,3},{68,4},{69,5},{70,6},{71,7},{72,8},{73... | collective-permute-start | bytes 12582920 | tf_op jit(solution)/shard_map/ppermute | solution.py:24
  335.9 5.5 copy-start.10
  335.9 5.5 copy-start.8
  345.1 4.5 copy-start.3
  349.6 6.2 %copy-start.11 = (bf16[1024,2048]{1,0:T(8,128)(2,1)S(1)}, bf16[1024,2048]{1,0:T(8,128)(2,1)}, u32[]{:S(2)}) copy-start(bf16[1024,2048]{1,0:T(8,128)(2,1)} %copy-done.10) | copy-start | bytes 12582916 | tf_op jit(solution)/shard_map/cond
  370.6 213.9 %reduce-scatter.5.cloned.1.call-start = ((), (), s32[]{:S(2)}) async-start(), calls=%async_computation.3 | async-start | bytes 17825792 | tf_op jit(solution)/shard_map/reduce_scatter | solution.py:172
Sparse Core Ops, SparseCore 0:
  370.7 30.2 reduce-scatter.2
  404.1 180.2 reduce-scatter.4
